TPU v7x, 32 devices: a whole 2x2x4 slice. The times are simulated.
32 devices in a mesh: req: 4 (over y, core), seq: 8 (over z, x).
Axes of the slice: x: 2, y: 2, z: 4, core: 2. Of those that a mesh axis runs over, the one named last changes fastest.
Arguments:
- embedded: bfloat16 [4, 48, 3584], P(None, 'req'), may hold values from -6 to 6
- cache_keys: bfloat16 [4, 4096, 2048], P('req', 'seq'), may hold values from -6 to 6
- cache_values: bfloat16 [4, 4096, 2048], P('req', 'seq'), may hold values from -6 to 6
- token_owner: int32 [4, 4096], P('req', 'seq'), may hold values from 0 to 11, as said below
- dealing: int32 [48], replicated, may hold values from 0 to 47, as said below
- lengths: int32 [48], replicated, may hold values from 1 to 2048, as said below
- project_weight: bfloat16 [3584, 8192], P(None, 'seq')
- output_weight: bfloat16 [4096, 3584], P('seq'), may hold values from -0.09375 to 0.09375
- gate_weight: bfloat16 [3584, 14336], P(None, ('req', 'seq')), may hold values from -0.09375 to 0.09375
- up_weight: bfloat16 [3584, 14336], P(None, ('req', 'seq')), may hold values from -0.09375 to 0.09375
- down_weight: bfloat16 [14336, 3584], P(('req', 'seq')), may hold values from -0.046875 to 0.046875
- gain_first: float32 [3584], replicated, may hold values from 0.1 to 1.9
- gain_second: float32 [3584], replicated, may hold values from 0.1 to 1.9
- gain_third: float32 [3584], replicated, may hold values from 0.1 to 1.9
- gain_fourth: float32 [3584], replicated, may hold values from 0.1 to 1.9
Outputs:
- results: bfloat16 [4, 48, 3584], P(None, 'req')
Inputs may be any that keep to these rules, and one draw needn't show every extreme that they name: A permutation of the requests; slot i of req group g serves request dealing[g * 12 + i]. The lengths of the 12 requests dealt to one group sum to 4096; in every group the longest is exactly 2048. `token_owner`: each slot owns a contiguous run of its group's pool, runs in slot order, as many tokens as its request's length.
All inputs are finite; a program needn't handle non-finite values.
Results may differ from a plain program's by a relative error of at most 0.012.
The roundings to bfloat16 on the way count: a program that leaves them out, or rounds other values in their place, can miss the bound.
Values may be sent and summed in bfloat16 or wider, within the bound.
A program may use at most 128 MiB of HBM per device.

v0:
```python
import math

import jax
import jax.numpy as jnp
from jax import lax
from jax.sharding import PartitionSpec as P

H = 16
KVH = 8
HD = 256
STEPS = 4


soft_cap = 50.0
epsilon = 1e-06


def rms_scale(values, gain):
    mean_square = jnp.mean(values * values, axis=-1, keepdims=True)
    return values * lax.rsqrt(mean_square + epsilon) * gain


def rotate(values, positions):
    half_width = values.shape[-1] // 2
    freq_index = jnp.arange(half_width, dtype=jnp.float32)
    inverse = jnp.exp(freq_index * (-2.0 * math.log(10000.0) / values.shape[-1]))
    angles = positions[:, None] * inverse[None, :]
    cosine = jnp.cos(angles)[:, None, :]
    sine = jnp.sin(angles)[:, None, :]
    first_half = values[..., :half_width]
    second_half = values[..., half_width:]
    return jnp.concatenate(
        [first_half * cosine - second_half * sine, second_half * cosine + first_half * sine],
        axis=-1,
    )


def capped_weight(scores):
    return jnp.exp(soft_cap * jnp.tanh(scores / soft_cap))


def rounded(values):
    return lax.optimization_barrier(values.astype(jnp.bfloat16)).astype(jnp.float32)


def body(
    embedded,
    cache_keys,
    cache_values,
    token_owner,
    dealing,
    lengths,
    project_weight,
    output_weight,
    gate_weight,
    up_weight,
    down_weight,
    gain_first,
    gain_second,
    gain_third,
    gain_fourth,
):
    row_count = embedded.shape[1]
    rows = STEPS * row_count
    width = embedded.shape[2]
    local_tokens = cache_keys.shape[1]
    value_width = cache_keys.shape[2]
    group_size = H // KVH
    attention_width = H * HD
    column_count = output_weight.shape[0]
    group_index = lax.axis_index("req")
    seq_index = lax.axis_index("seq")
    seq_size = lax.axis_size("seq")
    req_size = lax.axis_size("req")
    column_start = seq_index * column_count
    slot_requests = lax.dynamic_slice_in_dim(dealing, group_index * row_count, row_count)
    matches = slot_requests[:, None] == jnp.arange(dealing.shape[0], dtype=jnp.int32)[None, :]
    base_positions = jnp.sum(jnp.where(matches, lengths[None, :], 0), axis=1)
    positions = base_positions[None, :] + jnp.arange(STEPS, dtype=jnp.int32)[:, None]
    positions = positions.reshape(rows).astype(jnp.float32)
    key_pool = cache_keys[0].reshape(local_tokens, KVH, HD)
    value_pool = cache_values[0].reshape(local_tokens, KVH, HD)
    slots = jnp.tile(jnp.arange(row_count, dtype=jnp.int32), STEPS)
    moments = jnp.repeat(jnp.arange(STEPS, dtype=jnp.int32), row_count)
    owned_mask = token_owner[0][None, :] == slots[:, None]
    stream = embedded.reshape(rows, width).astype(jnp.float32)
    normed = rms_scale(stream, gain_first).astype(jnp.bfloat16)
    local_part = jnp.dot(normed, project_weight, preferred_element_type=jnp.float32).astype(
        jnp.bfloat16
    )
    projected = lax.all_gather(local_part, "seq", axis=1, tiled=True)
    query_rows = projected[:, :attention_width].astype(jnp.float32).reshape(rows, H, HD)
    queries = (rotate(query_rows, positions) * HD ** (-0.5)).astype(jnp.bfloat16)
    key_rows = (
        projected[:, attention_width : attention_width + value_width]
        .astype(jnp.float32)
        .reshape(rows, KVH, HD)
    )
    fresh_keys = rotate(key_rows, positions).astype(jnp.bfloat16)
    fresh_values = projected[:, attention_width + value_width :].reshape(rows, KVH, HD)
    grouped = queries.reshape(rows, KVH, group_size, HD)
    all_keys = jnp.concatenate([key_pool, fresh_keys], axis=0)
    all_values = jnp.concatenate([value_pool, fresh_values], axis=0)
    fresh_mask = (
        (slots[None, :] == slots[:, None])
        & (moments[None, :] <= moments[:, None])
        & (seq_index == 0)
    )
    mask = jnp.concatenate([owned_mask, fresh_mask], axis=1)
    scores = jnp.einsum("igqd,tgd->igqt", grouped, all_keys, preferred_element_type=jnp.float32)
    weights = jnp.where(mask[:, None, None, :], capped_weight(scores), 0.0)
    totals = lax.psum(jnp.sum(weights, axis=-1), "seq").reshape(rows, H)
    outputs = jnp.einsum(
        "igqt,tgd->igqd",
        weights.astype(jnp.bfloat16),
        all_values,
        preferred_element_type=jnp.float32,
    ).reshape(rows, attention_width)
    outputs = lax.psum_scatter(outputs, "seq", scatter_dimension=1, tiled=True)
    spread = jnp.repeat(totals, HD, axis=1)
    spread = lax.dynamic_slice_in_dim(spread, column_start, column_count, 1)
    attended = (outputs / spread).astype(jnp.bfloat16)
    partial = jnp.dot(attended, output_weight, preferred_element_type=jnp.float32)
    mixed = lax.psum(partial, "seq")
    middle = stream + rms_scale(mixed, gain_second)
    feed_input = rms_scale(middle, gain_third).astype(jnp.bfloat16)
    block_rows = lax.all_gather(feed_input, "req", axis=0, tiled=True)
    gate_part = jnp.dot(block_rows, gate_weight, preferred_element_type=jnp.float32)
    up_part = jnp.dot(block_rows, up_weight, preferred_element_type=jnp.float32)
    hidden = (jax.nn.gelu(gate_part, approximate=True) * up_part).astype(jnp.bfloat16)
    summed = jnp.dot(hidden, down_weight, preferred_element_type=jnp.float32)
    summed = lax.psum_scatter(summed, "req", scatter_dimension=0, tiled=True)
    summed = lax.psum(summed, "seq")
    results = (middle + rms_scale(summed, gain_fourth)).astype(jnp.bfloat16)
    return results.reshape(STEPS, row_count, width)


def solution(mesh):
    return jax.shard_map(
        body,
        mesh=mesh,
        in_specs=(
            P(None, "req", None),
            P("req", "seq", None),
            P("req", "seq", None),
            P("req", "seq"),
            P(),
            P(),
            P(None, "seq"),
            P("seq", None),
            P(None, ("req", "seq")),
            P(None, ("req", "seq")),
            P(("req", "seq"), None),
            P(),
            P(),
            P(),
            P(),
        ),
        out_specs=P(None, "req", None),
        check_vma=False,
    )
```

profile of v0, /device:TPU:0, one launch (start us, length us, event | category | flops | bytes accessed | tf_op | source)
XLA Modules:
  0.0 383.3 jit_solution(17114336762805842567)
XLA Ops:
  6.6 2.1 copy.64
  8.7 1.2 multiply_reduce_fusion.3
  9.9 2.1 reshape.160
  12.2 4.8 %convolution_convert_fusion = bf16[48,1024]{1,0:T(8,128)(2,1)S(1)} fusion(bf16[3584,1024]{1,0:T(8,128)(2,1)} %param.21, f32[48,3584]{1,0:T(8,128)} %reshape.160, f32[3584]{0:T(1024)S(1)} %copy-done.4, f32[48]{0:T(128)S(1)} %rsqrt.36), kind=kOutput, calls=%fused_computation.14 | convolution fusion | flops 352886784 | bytes 8140992 | tf_op jit(solution)/shard_map/dot_general | solution.py:88
  17.0 33.8 %all_gather.6 = bf16[48,8192]{1,0:T(8,128)(2,1)S(1)} all-gather(bf16[48,1024]{1,0:T(8,128)(2,1)S(1)} %convolution_convert_fusion), channel_id=1, replica_groups=mesh['req'=4,'seq'=8] {'seq'}, dimensions={1}, use_global_device_ids=true | all-gather | bytes 884736 | tf_op jit(solution)/shard_map/all_gather | solution.py:91
  51.7 0.9 slice_convert_fusion
  53.1 1.1 copy.83
  54.9 1.4 copy.84
  58.6 3.9 %copy.69 = bf16[1,512,2048]{1,2,0:T(8,128)(2,1)} copy(bf16[1,512,2048]{2,1,0:T(8,128)(2,1)} %param.16) | data formatting | bytes 4194304 | tf_op args[1]
  62.6 3.9 %copy.72 = bf16[512,8,256]{2,0,1:T(8,128)(2,1)} copy(bf16[512,8,256]{0,2,1:T(8,128)(2,1)} %bitcast.44) | data formatting | bytes 4194304 | tf_op jit(solution)/shard_map/reshape;squeeze | solution.py:81
  66.5 1.6 copy.92
  68.1 3.9 %copy.65 = bf16[1,512,2048]{1,2,0:T(8,128)(2,1)} copy(bf16[1,512,2048]{2,1,0:T(8,128)(2,1)} %param.17) | data formatting | bytes 4194304 | tf_op args[2]
  72.0 3.9 %copy.67 = bf16[512,8,256]{2,0,1:T(8,128)(2,1)} copy(bf16[512,8,256]{0,2,1:T(8,128)(2,1)} %bitcast.45) | data formatting | bytes 4194304 | tf_op jit(solution)/shard_map/reshape;squeeze | solution.py:82
  76.0 1.0 subtract_convert_fusion
  77.0 2.9 fusion.40
  80.5 1.5 copy.75
  82.1 2.6 reshape.156
  84.8 21.7 %psum.21 = f32[48,16]{0,1:T(8,128)S(1)} all-reduce(f32[48,16]{0,1:T(8,128)S(1)} %bitcast.56), channel_id=1, replica_groups=mesh['req'=4,'seq'=8] {'seq'}, use_global_device_ids=true, to_apply=%region_4.5 | all-reduce | flops 768 | bytes 6144 | tf_op jit(solution)/shard_map/psum | solution.py:112
  106.7 1.4 copy.85
  108.1 40.9 %reduce-scatter.3.cloned.1.call-done = f32[48,512]{1,0:T(8,128)} async-done(((f32[48,4096]{1,0:T(8,128)}), f32[48,512]{1,0:T(8,128)}) %reduce-scatter.3.cloned.1.call-update) | async-done | bytes 98320 | tf_op jit(solution)/shard_map/reduce_scatter | solution.py:119
  149.0 3.8 fusion.29
  152.8 72.8 %all-reduce.3.cloned.1.call-done = f32[48,3584]{1,0:T(8,128)} async-done(((f32[48,3584]{1,0:T(8,128)}), f32[48,3584]{1,0:T(8,128)}) %all-reduce.3.cloned.1.call-update) | async-done | bytes 688144 | tf_op jit(solution)/shard_map/psum | solution.py:124
  225.6 1.2 multiply_reduce_fusion.2
  226.9 1.6 multiply_reduce_fusion.1
  230.3 17.7 %all-gather.2.cloned.1.call-done = bf16[192,3584]{1,0:T(8,128)(2,1)} async-done(((bf16[48,3584]{1,0:T(8,128)(2,1)}), bf16[192,3584]{1,0:T(8,128)(2,1)}) %all-gather.2.cloned.1.call-update) | async-done | bytes 1376272 | tf_op jit(solution)/shard_map/all_gather | solution.py:127
  247.9 4.1 %fusion.41 = f32[192,448]{1,0:T(8,128)} fusion(bf16[192,3584]{1,0:T(8,128)(2,1)} %all-gather.2.cloned.1.call-done, bf16[3584,448]{0,1:T(8,128)(2,1)} %param.23), kind=kOutput, calls=%fused_computation.75 | convolution fusion | flops 616562688 | bytes 4931584 | tf_op jit(solution)/shard_map/dot_general | solution.py:128
  252.1 6.0 %fusion.10 = f32[192,3584]{1,0:T(8,128)} fusion(bf16[448,3584]{1,0:T(8,128)(2,1)S(1)} %copy-done, bf16[192,3584]{1,0:T(8,128)(2,1)} %all-gather.2.cloned.1.call-done, bf16[3584,448]{0,1:T(8,128)(2,1)} %param.24, f32[192,448]{1,0:T(8,128)} %fusion.41), kind=kOutput, calls=%fused_computation.15 | convolution fusion | flops 1233985536 | bytes 10895360 | tf_op jit(solution)/shard_map/dot_general | solution.py:131
  258.2 35.6 %reduce-scatter.5.cloned.1.call-done = f32[48,3584]{1,0:T(8,128)} async-done(((f32[192,3584]{1,0:T(8,128)}), f32[48,3584]{1,0:T(8,128)}) %reduce-scatter.5.cloned.1.call-update) | async-done | bytes 688144 | tf_op jit(solution)/shard_map/reduce_scatter | solution.py:132
  293.8 77.4 %all-reduce.5.cloned.1.call-done = f32[48,3584]{1,0:T(8,128)} async-done(((f32[48,3584]{1,0:T(8,128)}), f32[48,3584]{1,0:T(8,128)}) %all-reduce.5.cloned.1.call-update) | async-done | bytes 688144 | tf_op jit(solution)/shard_map/psum | solution.py:133
  371.1 1.2 multiply_reduce_fusion
  372.4 1.5 add_convert_fusion
  374.7 2.0 copy.77
  (60 shorter events, 8.2 us)
Async XLA Ops:
  6.5 245.5 %copy-start = (bf16[448,3584]{1,0:T(8,128)(2,1)S(1)}, bf16[448,3584]{1,0:T(8,128)(2,1)}, u32[]{:S(2)}) copy-start(bf16[448,3584]{1,0:T(8,128)(2,1)} %param.25) | copy-start | bytes 9633796
  6.5 5.7 %copy-start.4 = (f32[3584]{0:T(1024)S(1)}, f32[3584]{0:T(1024)}, u32[]{:S(2)}) copy-start(f32[3584]{0:T(1024)} %param.26) | copy-start | bytes 43012
  6.5 142.4 %reduce-scatter.3.cloned.1.call-start = ((), (), s32[]{:S(2)}) async-start(), calls=%async_computation.2 | async-start | bytes 884736 | tf_op jit(solution)/shard_map/reduce_scatter | solution.py:119
  17.0 35.6 %copy-start.8 = (s32[48]{0:T(128)S(1)}, s32[48]{0:T(128)}, u32[]{:S(2)}) copy-start(s32[48]{0:T(128)} %param.19) | copy-start | bytes 580
  17.0 35.7 %copy-start.9 = (s32[48]{0:T(128)S(1)}, s32[48]{0:T(128)}, u32[]{:S(2)}) copy-start(s32[48]{0:T(128)} %param.20) | copy-start | bytes 580
  54.9 3.6 copy-start.7
  77.0 2.9 copy-start.2
  77.0 2.9 copy-start.3
  84.7 140.9 %all-reduce.3.cloned.1.call-start = ((), (), s32[]{:S(2)}) async-start(), calls=%async_computation.3 | async-start | bytes 1376256 | tf_op jit(solution)/shard_map/psum | solution.py:124
  149.0 77.9 %copy-start.6 = (f32[3584]{0:T(1024)S(1)}, f32[3584]{0:T(1024)}, u32[]{:S(2)}) copy-start(f32[3584]{0:T(1024)} %param.27) | copy-start | bytes 43012
  152.7 76.6 %copy-start.5 = (f32[3584]{0:T(1024)S(1)}, f32[3584]{0:T(1024)}, u32[]{:S(2)}) copy-start(f32[3584]{0:T(1024)} %param.28) | copy-start | bytes 43012
  152.7 95.2 %all-gather.2.cloned.1.call-start = ((), (), s32[]{:S(2)}) async-start(), calls=%async_computation.4 | async-start | bytes 1720320 | tf_op jit(solution)/shard_map/all_gather | solution.py:127
  228.4 0.9 copy-start.1
  230.2 63.5 %reduce-scatter.5.cloned.1.call-start = ((), (), s32[]{:S(2)}) async-start(), calls=%async_computation.5 | async-start | bytes 3440640 | tf_op jit(solution)/shard_map/reduce_scatter | solution.py:132
  258.1 113.0 %all-reduce.5.cloned.1.call-start = ((), (), s32[]{:S(2)}) async-start(), calls=%async_computation.6 | async-start | bytes 1376256 | tf_op jit(solution)/shard_map/psum | solution.py:133
Sparse Core Ops, SparseCore 0:
  84.8 64.0 reduce-scatter.2
  152.9 72.6 all-reduce.2
  230.3 17.5 all-gather.1
  258.2 35.4 reduce-scatter.4
  297.4 73.6 all-reduce.4
where the time goes:
time: 384 us; the launch traced here: 383 us
  waiting for transfers between devices  244 us (64%)
  blocking collectives  55.5 us (14%)
  local copies, waits for them, and re-layouts  36.6 us (10%)
  matrix products  22.2 us (6%)
  between operations  13.3 us (3%)
  other arithmetic  11.1 us (3%)
    psum x1, waiting for transfers between devices, body(): summed = lax.psum(summed, 'seq')  77.4 us
    psum x1, waiting for transfers between devices, body(): mixed = lax.psum(partial, 'seq')  72.8 us
    reduce_scatter x1, waiting for transfers between devices, body(): outputs = lax.psum_scatter(outputs, 'seq', scatter_dimension=1, tiled=True)  40.9 us
    reduce_scatter x1, waiting for transfers between devices, body(): summed = lax.psum_scatter(summed, 'req', scatter_dimension=0, tiled=True)  35.6 us
    all_gather x1, blocking collectives, body(): projected = lax.all_gather(local_part, 'seq', axis=1, tiled=True)  33.8 us
    psum x1, blocking collectives, body(): totals = lax.psum(jnp.sum(weights, axis=-1), 'seq').reshape(rows, H)  21.7 us
    all_gather x1, waiting for transfers between devices, body(): block_rows = lax.all_gather(feed_input, 'req', axis=0, tiled=True)  17.7 us
    unnamed x26, local copies, waits for them, and re-layouts  12.7 us
  transfers between devices with their start and end apart: 5, of which 5 were waited for; matrix products, arithmetic and copies ran while one was open for 0% of the time, Pallas kernels for 0%

commit v1 on v0

--- a/solution.py
+++ b/solution.py
@@ -3,6 +3,8 @@
 import jax
 import jax.numpy as jnp
 from jax import lax
+from jax.experimental import pallas as pl
+from jax.experimental.pallas import tpu as pltpu
 from jax.sharding import PartitionSpec as P
 
 H = 16
@@ -43,7 +45,7 @@
     return lax.optimization_barrier(values.astype(jnp.bfloat16)).astype(jnp.float32)
 
 
-def body(
+def plain_body(
     embedded,
     cache_keys,
     cache_values,
@@ -135,6 +137,485 @@
     return results.reshape(STEPS, row_count, width)
 
 
+MESH = pl.DeviceIdType.MESH
+SEQ = 8
+REQ = 4
+OWNERS = 6
+TILE = 8
+MIX_CHUNKS = 2
+SUM_CHUNKS = 4
+
+
+def kernel(
+    x_ref, cos_ref, sin_ref, mask_ref, fresh_mask_ref, g1_ref, g2_ref, g3_ref, g4_ref,
+    pw_hbm, ck_hbm, cv_hbm, ow_hbm, gw_hbm, uw_hbm, dw_hbm,
+    out_ref,
+    pw, ck, cv, ow, gw, uw, dw,
+    gbuf, bsend, brecv, tot_ref, tsend, trecv, csend, crecv, mid_ref, feed, lhs_ref, hid_ref,
+    part_ref, e1send, e1recv, e2send, e2recv, e3send, e3recv,
+    load_sem, a_send, a_recv, b_send, b_recv, t_send, t_recv, c_send, c_recv,
+    d_send, d_recv, d2_send, d2_recv, e1_ssem, e1_rsem, e2_ssem, e2_rsem, e3_ssem, e3_rsem,
+    f_send, f_recv,
+):
+    me = lax.axis_index("seq")
+    row = lax.axis_index("req")
+    width = x_ref.shape[2]
+    rows = OWNERS * TILE
+    ff = gw.shape[1]
+    other_core = row + 1 - 2 * lax.rem(row, 2)
+    other_y = lax.rem(row + 2, REQ)
+    is_owner = (me >= 1) & (me <= OWNERS)
+    mine = jnp.minimum(jnp.maximum(me - 1, 0), OWNERS - 1)
+
+    loads = [
+        pltpu.make_async_copy(src, dst, load_sem.at[n])
+        for n, (src, dst) in enumerate(
+            [(pw_hbm, pw), (ck_hbm, ck), (cv_hbm, cv), (ow_hbm, ow), (gw_hbm, gw), (uw_hbm, uw)]
+        )
+    ]
+    dw[ff:, :] = jnp.zeros((dw.shape[0] - ff, width), dw.dtype)
+    hid_ref[...] = jnp.zeros_like(hid_ref)
+    loads.append(pltpu.make_async_copy(dw_hbm, dw.at[pl.ds(0, ff)], load_sem.at[6]))
+    for load in loads:
+        load.start()
+
+    barrier = pltpu.get_barrier_semaphore()
+    for d in range(1, SEQ):
+        pl.semaphore_signal(
+            barrier, inc=1, device_id={"seq": lax.rem(me + d, SEQ)}, device_id_type=MESH
+        )
+    pl.semaphore_signal(barrier, inc=1, device_id={"req": other_core}, device_id_type=MESH)
+    pl.semaphore_signal(barrier, inc=1, device_id={"req": other_y}, device_id_type=MESH)
+
+    def remote(src, dst, send, recv, target):
+        return pltpu.make_async_remote_copy(
+            src_ref=src, dst_ref=dst, send_sem=send, recv_sem=recv,
+            device_id=target, device_id_type=MESH,
+        )
+
+    def rms(values, gain):
+        mean_square = jnp.mean(values * values, axis=-1, keepdims=True)
+        return values * lax.rsqrt(mean_square + epsilon) * gain
+
+    stream = x_ref[...].astype(jnp.float32).reshape(rows, width)
+    normed = rms(stream, g1_ref[...]).astype(jnp.bfloat16)
+    loads[0].wait()
+    projected = jnp.dot(normed, pw[...], preferred_element_type=jnp.float32)
+    projected = projected.astype(jnp.bfloat16).astype(jnp.float32)
+    cosine, sine = cos_ref[...], sin_ref[...]
+    half = HD // 2
+    for h in range(pw.shape[1] // HD):
+        a = projected[:, h * HD : h * HD + half]
+        b = projected[:, h * HD + half : (h + 1) * HD]
+        gbuf[me, :, h * HD : h * HD + half] = (a * cosine - b * sine).astype(jnp.bfloat16)
+        gbuf[me, :, h * HD + half : (h + 1) * HD] = (b * cosine + a * sine).astype(jnp.bfloat16)
+    pl.semaphore_wait(barrier, SEQ + 1)
+
+    def a_copy(d):
+        return remote(
+            gbuf.at[me], gbuf.at[me], a_send.at[d - 1], a_recv.at[me],
+            {"seq": lax.rem(me + d, SEQ)},
+        )
+
+    for d in range(1, SEQ):
+        a_copy(d).start()
+    for d in range(1, SEQ):
+        source = lax.rem(me + d, SEQ)
+        remote(
+            gbuf.at[source], gbuf.at[source], a_send.at[d - 1], a_recv.at[source], {"seq": source}
+        ).wait_recv()
+
+    loads[1].wait()
+    loads[2].wait()
+    owned = mask_ref[...] > 0.5
+    lanes = lax.broadcasted_iota(jnp.int32, (2 * rows, 128), 1)
+    totals = jnp.zeros((2 * rows, 128), jnp.float32)
+
+    def attend(queries, keys, values, allowed):
+        scores = lax.dot_general(
+            queries, keys, (((1,), (1,)), ((), ())), preferred_element_type=jnp.float32
+        )
+        weights = jnp.where(allowed, capped_weight(scores), 0.0)
+        outputs = jnp.dot(
+            weights.astype(jnp.bfloat16), values, preferred_element_type=jnp.float32
+        )
+        return jnp.sum(weights, axis=-1, keepdims=True), outputs
+
+    def b_copy(j):
+        return remote(
+            bsend.at[j - 1], brecv.at[j - 1], b_send.at[j - 1], b_recv.at[j - 1],
+            {"seq": lax.rem(me + j, SEQ)},
+        )
+
+    def t_copy(j):
+        return remote(
+            tsend, trecv.at[j - 1], t_send.at[j - 1], t_recv.at[j - 1],
+            {"seq": lax.rem(me + j, SEQ)},
+        )
+
+    for j in range(1, SEQ + 1):
+        e = lax.rem(me + j, SEQ)
+        block = e // 2
+        first = pl.multiple_of(lax.rem(e, 2) * (2 * HD), 2 * HD)
+        queries = jnp.concatenate(
+            [gbuf[block, :, pl.ds(first, HD)], gbuf[block, :, pl.ds(first + HD, HD)]], axis=0
+        )
+        head = pl.ds(pl.multiple_of(e * HD, HD), HD)
+        total, outputs = attend(queries, ck[:, head], cv[:, head], owned)
+        if j < SEQ:
+            bsend[j - 1] = outputs.astype(jnp.bfloat16)
+            b_copy(j).start()
+        else:
+            fresh = pl.ds(pl.multiple_of(lax.rem(e, 4) * HD, HD), HD)
+            fresh_total, fresh_outputs = attend(
+                queries, gbuf[4 + e // 4, :, fresh], gbuf[6 + e // 4, :, fresh],
+                fresh_mask_ref[...] > 0.5,
+            )
+            total = total + fresh_total
+            outputs = outputs + fresh_outputs
+        totals = totals + jnp.where(lanes == e, total, 0.0)
+    tot_ref[2 * rows :, :] = jnp.zeros((128 - 2 * rows, 128), jnp.float32)
+    tot_ref[: 2 * rows, :] = totals
+    tsend[...] = tot_ref[...].T[:KVH]
+    for j in range(1, SEQ):
+        t_copy(j).start()
+    everyone = tsend[...]
+    for j in range(1, SEQ):
+        b_copy(j).wait_recv()
+        t_copy(j).wait_recv()
+        outputs = outputs + brecv[j - 1].astype(jnp.float32)
+        everyone = everyone + trecv[j - 1]
+    tot_ref[...] = jnp.zeros((128, 128), jnp.float32)
+    tot_ref[:KVH, :] = everyone
+    spread = tot_ref[...].T
+    column = jnp.sum(jnp.where(lanes == me, spread[: 2 * rows], 0.0), axis=-1, keepdims=True)
+    attended = outputs / column
+    attended = jnp.concatenate([attended[:rows], attended[rows:]], axis=1).astype(jnp.bfloat16)
+
+    loads[3].wait()
+    mix = width // MIX_CHUNKS
+
+    def c_send_to(c, d):
+        target = lax.rem(me + d, SEQ)
+        owner = jnp.minimum(jnp.maximum(target - 1, 0), OWNERS - 1)
+        copy = remote(
+            csend.at[c, owner], crecv.at[c, d - 1], c_send.at[c, d - 1], c_recv.at[c, d - 1],
+            {"seq": target},
+        )
+        return (target >= 1) & (target <= OWNERS), copy
+
+    for c in range(MIX_CHUNKS):
+        part = jnp.dot(
+            attended, ow[:, c * mix : (c + 1) * mix], preferred_element_type=jnp.float32
+        )
+        csend[c] = part.reshape(OWNERS, TILE, mix).astype(jnp.bfloat16)
+        for d in range(1, SEQ):
+            pred, copy = c_send_to(c, d)
+            pl.when(pred)(copy.start)
+
+    def d_copy(d):
+        return remote(
+            feed.at[0, mine], feed.at[0, mine], d_send.at[d - 1], d_recv.at[mine],
+            {"seq": lax.rem(me + d, SEQ)},
+        )
+
+    @pl.when(is_owner)
+    def _():
+        pieces = []
+        for c in range(MIX_CHUNKS):
+            piece = csend[c, mine].astype(jnp.float32)
+            for d in range(1, SEQ):
+                c_send_to(c, d)[1].wait_recv()
+                piece = piece + crecv[c, d - 1].astype(jnp.float32)
+            pieces.append(piece)
+        mixed = jnp.concatenate(pieces, axis=1)
+        middle = x_ref[mine].astype(jnp.float32) + rms(mixed, g2_ref[...])
+        mid_ref[...] = middle
+        feed[0, mine] = rms(middle, g3_ref[...]).astype(jnp.bfloat16)
+        for d in range(1, SEQ):
+            d_copy(d).start()
+
+    def to_y(o):
+        return remote(
+            feed.at[0, o], feed.at[2, o], d2_send.at[0, o], d2_recv.at[0, o], {"req": other_y}
+        )
+
+    def to_core(o):
+        return remote(
+            feed.at[0, o], feed.at[1, o], d2_send.at[1, o], d2_recv.at[1, o], {"req": other_core}
+        )
+
+    def to_corner(o):
+        return remote(
+            feed.at[2, o], feed.at[3, o], d2_send.at[2, o], d2_recv.at[2, o], {"req": other_core}
+        )
+
+    for o in range(OWNERS):
+        @pl.when(me != o + 1)
+        def _():
+            remote(
+                feed.at[0, o], feed.at[0, o], d_send.at[0], d_recv.at[o], {"seq": o + 1}
+            ).wait_recv()
+
+        to_y(o).start()
+        to_core(o).start()
+    for o in range(OWNERS):
+        to_y(o).wait_recv()
+        to_corner(o).start()
+    for o in range(OWNERS):
+        to_core(o).wait_recv()
+        to_corner(o).wait_recv()
+
+    for q in range(REQ):
+        lhs_ref[q * rows : (q + 1) * rows, :] = (
+            feed[q].astype(jnp.float32).reshape(rows, width).astype(jnp.bfloat16)
+        )
+    loads[4].wait()
+    loads[5].wait()
+    gate_part = jnp.dot(lhs_ref[...], gw[...], preferred_element_type=jnp.float32)
+    up_part = jnp.dot(lhs_ref[...], uw[...], preferred_element_type=jnp.float32)
+    hidden = (jax.nn.gelu(gate_part, approximate=True) * up_part).astype(jnp.bfloat16)
+    hid_ref[:, :ff] = hidden
+    loads[6].wait()
+    piece_width = width // SUM_CHUNKS
+
+    def e1_copy(c):
+        return remote(
+            e1send.at[c], e1recv.at[c], e1_ssem.at[c], e1_rsem.at[c], {"req": other_core}
+        )
+
+    def e2_copy(c):
+        return remote(e2send.at[c], e2recv.at[c], e2_ssem.at[c], e2_rsem.at[c], {"req": other_y})
+
+    def e3_copy(c, d):
+        target = lax.rem(me + d, SEQ)
+        owner = jnp.minimum(jnp.maximum(target - 1, 0), OWNERS - 1)
+        copy = remote(
+            e3send.at[c, owner], e3recv.at[c, d - 1], e3_ssem.at[c, d - 1], e3_rsem.at[c, d - 1],
+            {"seq": target},
+        )
+        return (target >= 1) & (target <= OWNERS), copy
+
+    for c in range(SUM_CHUNKS):
+        part = jnp.dot(
+            hid_ref[...],
+            dw[:, c * piece_width : (c + 1) * piece_width],
+            preferred_element_type=jnp.float32,
+        )
+        e1send[c, :rows] = part[rows : 2 * rows].astype(jnp.bfloat16)
+        e1send[c, rows:] = part[3 * rows :].astype(jnp.bfloat16)
+        part_ref[c, :rows] = part[:rows]
+        part_ref[c, rows:] = part[2 * rows : 3 * rows]
+        e1_copy(c).start()
+    for c in range(SUM_CHUNKS):
+        e1_copy(c).wait_recv()
+        e2send[c] = (part_ref[c, rows:] + e1recv[c, rows:].astype(jnp.float32)).astype(
+            jnp.bfloat16
+        )
+        e2_copy(c).start()
+    for c in range(SUM_CHUNKS):
+        e2_copy(c).wait_recv()
+        kept = part_ref[c, :rows] + e1recv[c, :rows].astype(jnp.float32)
+        kept = kept + e2recv[c].astype(jnp.float32)
+        e3send[c] = kept.reshape(OWNERS, TILE, piece_width).astype(jnp.bfloat16)
+        for d in range(1, SEQ):
+            pred, copy = e3_copy(c, d)
+            pl.when(pred)(copy.start)
+
+    def f_copy(d):
+        return remote(
+            out_ref.at[mine], out_ref.at[mine], f_send.at[d - 1], f_recv.at[mine],
+            {"seq": lax.rem(me + d, SEQ)},
+        )
+
+    @pl.when(is_owner)
+    def _():
+        pieces = []
+        for c in range(SUM_CHUNKS):
+            piece = e3send[c, mine].astype(jnp.float32)
+            for d in range(1, SEQ):
+                e3_copy(c, d)[1].wait_recv()
+                piece = piece + e3recv[c, d - 1].astype(jnp.float32)
+            pieces.append(piece)
+        summed = jnp.concatenate(pieces, axis=1)
+        out_ref[mine] = (mid_ref[...] + rms(summed, g4_ref[...])).astype(jnp.bfloat16)
+        for d in range(1, SEQ):
+            f_copy(d).start()
+
+    for o in range(OWNERS):
+        @pl.when(me != o + 1)
+        def _():
+            remote(
+                out_ref.at[o], out_ref.at[o], f_send.at[0], f_recv.at[o], {"seq": o + 1}
+            ).wait_recv()
+
+    for d in range(1, SEQ):
+        a_copy(d).wait_send()
+        b_copy(d).wait_send()
+        t_copy(d).wait_send()
+        for c in range(MIX_CHUNKS):
+            pred, copy = c_send_to(c, d)
+            pl.when(pred)(copy.wait_send)
+        for c in range(SUM_CHUNKS):
+            pred, copy = e3_copy(c, d)
+            pl.when(pred)(copy.wait_send)
+    for o in range(OWNERS):
+        to_y(o).wait_send()
+        to_core(o).wait_send()
+        to_corner(o).wait_send()
+    for c in range(SUM_CHUNKS):
+        e1_copy(c).wait_send()
+        e2_copy(c).wait_send()
+
+    @pl.when(is_owner)
+    def _():
+        for d in range(1, SEQ):
+            d_copy(d).wait_send()
+            f_copy(d).wait_send()
+
+
+def fused_body(
+    embedded,
+    cache_keys,
+    cache_values,
+    token_owner,
+    dealing,
+    lengths,
+    project_weight,
+    output_weight,
+    gate_weight,
+    up_weight,
+    down_weight,
+    gain_first,
+    gain_second,
+    gain_third,
+    gain_fourth,
+):
+    row_count = embedded.shape[1]
+    rows = STEPS * row_count
+    width = embedded.shape[2]
+    tokens = cache_keys.shape[1]
+    kvw = cache_keys.shape[2]
+    columns = project_weight.shape[1]
+    depth = output_weight.shape[0]
+    ff = gate_weight.shape[1]
+    ff_pad = -(-ff // 128) * 128
+    mix = width // MIX_CHUNKS
+    piece = width // SUM_CHUNKS
+    group_index = lax.axis_index("req")
+    seq_index = lax.axis_index("seq")
+    slot_requests = lax.dynamic_slice_in_dim(dealing, group_index * row_count, row_count)
+    matches = slot_requests[:, None] == jnp.arange(dealing.shape[0], dtype=jnp.int32)[None, :]
+    base_positions = jnp.sum(jnp.where(matches, lengths[None, :], 0), axis=1)
+    positions = base_positions[None, :] + jnp.arange(STEPS, dtype=jnp.int32)[:, None]
+    positions = positions.reshape(rows).astype(jnp.float32)
+    freq_index = jnp.arange(HD // 2, dtype=jnp.float32)
+    inverse = jnp.exp(freq_index * (-2.0 * math.log(10000.0) / HD))
+    angles = positions[:, None] * inverse[None, :]
+    scale = jnp.where(seq_index < SEQ // 2, HD ** (-0.5), 1.0)
+    turned = seq_index < 3 * SEQ // 4
+    cosine = jnp.where(turned, jnp.cos(angles) * scale, 1.0)
+    sine = jnp.where(turned, jnp.sin(angles) * scale, 0.0)
+    slots = jnp.tile(jnp.arange(row_count, dtype=jnp.int32), STEPS)
+    moments = jnp.repeat(jnp.arange(STEPS, dtype=jnp.int32), row_count)
+    mask = (token_owner[0][None, :] == jnp.tile(slots, 2)[:, None]).astype(jnp.float32)
+    fresh_mask = (slots[None, :] == slots[:, None]) & (moments[None, :] <= moments[:, None])
+    fresh_mask = jnp.tile(fresh_mask, (2, 1)).astype(jnp.float32)
+    bf16, f32 = jnp.bfloat16, jnp.float32
+    dma = pltpu.SemaphoreType.DMA
+    vmem = pl.BlockSpec(memory_space=pltpu.VMEM)
+    hbm = pl.BlockSpec(memory_space=pl.ANY)
+    out = pl.pallas_call(
+        kernel,
+        out_shape=jax.ShapeDtypeStruct((OWNERS, TILE, width), bf16),
+        in_specs=[vmem] * 9 + [hbm] * 7,
+        out_specs=vmem,
+        scratch_shapes=[
+            pltpu.VMEM((width, columns), bf16),
+            pltpu.VMEM((tokens, kvw), bf16),
+            pltpu.VMEM((tokens, kvw), bf16),
+            pltpu.VMEM((depth, width), bf16),
+            pltpu.VMEM((width, ff), bf16),
+            pltpu.VMEM((width, ff), bf16),
+            pltpu.VMEM((ff_pad, width), bf16),
+            pltpu.VMEM((SEQ, rows, columns), bf16),
+            pltpu.VMEM((SEQ - 1, 2 * rows, HD), bf16),
+            pltpu.VMEM((SEQ - 1, 2 * rows, HD), bf16),
+            pltpu.VMEM((128, 128), f32),
+            pltpu.VMEM((KVH, 128), f32),
+            pltpu.VMEM((SEQ - 1, KVH, 128), f32),
+            pltpu.VMEM((MIX_CHUNKS, OWNERS, TILE, mix), bf16),
+            pltpu.VMEM((MIX_CHUNKS, SEQ - 1, TILE, mix), bf16),
+            pltpu.VMEM((TILE, width), f32),
+            pltpu.VMEM((REQ, OWNERS, TILE, width), bf16),
+            pltpu.VMEM((REQ * rows, width), bf16),
+            pltpu.VMEM((REQ * rows, ff_pad), bf16),
+            pltpu.VMEM((SUM_CHUNKS, 2 * rows, piece), f32),
+            pltpu.VMEM((SUM_CHUNKS, 2 * rows, piece), bf16),
+            pltpu.VMEM((SUM_CHUNKS, 2 * rows, piece), bf16),
+            pltpu.VMEM((SUM_CHUNKS, rows, piece), bf16),
+            pltpu.VMEM((SUM_CHUNKS, rows, piece), bf16),
+            pltpu.VMEM((SUM_CHUNKS, OWNERS, TILE, piece), bf16),
+            pltpu.VMEM((SUM_CHUNKS, SEQ - 1, TILE, piece), bf16),
+            dma((7,)),
+            dma((SEQ - 1,)),
+            dma((SEQ,)),
+            dma((SEQ - 1,)),
+            dma((SEQ - 1,)),
+            dma((SEQ - 1,)),
+            dma((SEQ - 1,)),
+            dma((MIX_CHUNKS, SEQ - 1)),
+            dma((MIX_CHUNKS, SEQ - 1)),
+            dma((SEQ - 1,)),
+            dma((OWNERS,)),
+            dma((3, OWNERS)),
+            dma((3, OWNERS)),
+            dma((SUM_CHUNKS,)),
+            dma((SUM_CHUNKS,)),
+            dma((SUM_CHUNKS,)),
+            dma((SUM_CHUNKS,)),
+            dma((SUM_CHUNKS, SEQ - 1)),
+            dma((SUM_CHUNKS, SEQ - 1)),
+            dma((SEQ - 1,)),
+            dma((OWNERS,)),
+        ],
+        compiler_params=pltpu.CompilerParams(
+            collective_id=0, has_side_effects=True, vmem_limit_bytes=58 << 20
+        ),
+    )(
+        embedded.reshape(OWNERS, TILE, width),
+        cosine,
+        sine,
+        mask,
+        fresh_mask,
+        gain_first[None, :],
+        gain_second[None, :],
+        gain_third[None, :],
+        gain_fourth[None, :],
+        project_weight,
+        cache_keys[0],
+        cache_values[0],
+        output_weight,
+        gate_weight,
+        up_weight,
+        down_weight,
+    )
+    return out.reshape(STEPS, row_count, width)
+
+
+def body(*args):
+    embedded, cache_keys = args[0], args[1]
+    rows = STEPS * embedded.shape[1]
+    fits = (
+        lax.axis_size("seq") == SEQ
+        and lax.axis_size("req") == REQ
+        and rows == OWNERS * TILE
+        and KVH == SEQ
+        and cache_keys.shape[2] == KVH * HD
+    )
+    return fused_body(*args) if fits else plain_body(*args)
+
+
 def solution(mesh):
     return jax.shard_map(
         body,

time: 384 us -> 116 us (0.30)
  waiting for transfers between devices: 244 us -> 0 us
  Pallas kernels: 0 us -> 90.4 us
  blocking collectives: 55.5 us -> 0 us
  matrix products: 22.2 us -> 0 us
  local copies, waits for them, and re-layouts: 36.6 us -> 20.5 us
  between operations: 13.3 us -> 0.04 us
  other arithmetic: 11.1 us -> 3.15 us
    psum x2 -> x0, waiting for transfers between devices: 150 us -> none  [the longest x1 77.4 us: body(): summed = lax.psum(summed, 'seq')]
    pallas_call x0 -> x1, Pallas kernels: none -> 90.4 us  [fused_body(): pl.pallas_call(kernel, out_shape=jax.ShapeDtypeStruct((OWNERS, TILE, widt...]
    reduce_scatter x2 -> x0, waiting for transfers between devices: 76.5 us -> none  [the longest x1 40.9 us: body(): outputs = lax.psum_scatter(outputs, 'seq', scatter_dimension=1, tiled=True)]
    all_gather x1 -> x0, blocking collectives: 33.8 us -> none  [body(): projected = lax.all_gather(local_part, 'seq', axis=1, tiled=True)]
    dot_general x6 -> x0, matrix products: 22.2 us -> none  [the longest x1 6.02 us: body(): summed = jnp.dot(hidden, down_weight, preferred_element_type=jnp.float32)]
    psum x1 -> x0, blocking collectives: 21.7 us -> none  [body(): totals = lax.psum(jnp.sum(weights, axis=-1), 'seq').reshape(rows, H)]
    all_gather x1 -> x0, waiting for transfers between devices: 17.7 us -> none  [body(): block_rows = lax.all_gather(feed_input, 'req', axis=0, tiled=True)]
    another operation x3 -> x4, local copies, waits for them, and re-layouts: 7.85 us -> 0.71 us  [the longest x1 0.62 us: fused_body(): fresh_mask = jnp.tile(fresh_mask, (2, 1)).astype(jnp.float32)]
  transfers between devices with their start and end apart: 5 -> 0, of which waited for: 5 -> 0; matrix products, arithmetic and copies ran while one was open for 0% -> 0% of each run, Pallas kernels for 0% -> 0%
where the time goes in v1:
time: 116 us; the launch traced here: 114 us
  Pallas kernels  90.4 us (78%)
  local copies, waits for them, and re-layouts  20.5 us (18%)
  other arithmetic  3.15 us (3%)
    pallas_call x1, Pallas kernels, fused_body(): pl.pallas_call(kernel, out_shape=jax.ShapeDtypeStruct((OWNERS, TILE, widt...  90.4 us
    unnamed x5, local copies, waits for them, and re-layouts  10.6 us

profile of v1, /device:TPU:0, one launch (start us, length us, event | category | flops | bytes accessed | tf_op | source)
XLA Modules:
  0.0 114.1 jit_solution(2667354773695578155)
XLA Ops:
  0.0 0.7 dynamic_slice.3
  0.7 0.8 select_reduce_fusion
  1.6 0.1 add.31
  1.7 0.1 tile.25
  1.8 0.1 eq.52
  1.9 0.1 add.33
  1.9 1.3 %broadcast_in_dim.43.g1_ref = f32[1,3584]{1,0:T(1,128)} reshape(f32[3584]{0:T(1024)} %param.26) | data formatting | bytes 28672 | tf_op jit(solution)/shard_map/broadcast_in_dim | solution.py:591
  3.3 1.3 %broadcast_in_dim.44.g2_ref = f32[1,3584]{1,0:T(1,128)} reshape(f32[3584]{0:T(1024)} %param.27) | data formatting | bytes 28672 | tf_op jit(solution)/shard_map/broadcast_in_dim | solution.py:592
  4.6 1.3 %broadcast_in_dim.45.g3_ref = f32[1,3584]{1,0:T(1,128)} reshape(f32[3584]{0:T(1024)} %param.28) | data formatting | bytes 28672 | tf_op jit(solution)/shard_map/broadcast_in_dim | solution.py:593
  5.9 1.3 %broadcast_in_dim.46.g4_ref = f32[1,3584]{1,0:T(1,128)} reshape(f32[3584]{0:T(1024)} %param.29) | data formatting | bytes 28672 | tf_op jit(solution)/shard_map/broadcast_in_dim | solution.py:594
  7.3 0.1 and_convert_fusion
  7.3 0.6 tile.27
  8.0 0.8 fusion.3
  8.7 1.4 %compare_convert_fusion.mask_ref = f32[96,512]{1,0:T(8,128)} fusion(s32[512]{0:T(512)} %bitcast.7, s32[96]{0:T(128)S(1)} %eq.52), kind=kLoop, calls=%fused_computation | loop fusion | flops 98304 | bytes 199040 | tf_op jit(solution)/shard_map/convert_element_type | solution.py:521
  10.2 1.0 copy.24
  11.2 0.8 reshape.97.x_ref
  12.0 0.0 copy-start
  12.0 5.9 %copy.25.gw_hbm = bf16[3584,448]{1,0:T(8,128)(2,1)} copy(bf16[3584,448]{0,1:T(8,128)(2,1)} %param.23) | data formatting | bytes 6422528 | tf_op args[8]
  17.9 0.0 copy-done
  17.9 3.7 %copy.26.uw_hbm = bf16[3584,448]{1,0:T(8,128)(2,1)} copy(bf16[3584,448]{0,1:T(8,128)(2,1)S(1)} %copy-done) | data formatting | bytes 6422528 | tf_op args[9]
  21.6 90.4 %shard_map.145 = bf16[6,8,3584]{2,1,0:T(8,128)(2,1)} custom-call(bf16[6,8,3584]{2,1,0:T(8,128)(2,1)} %reshape.97.x_ref, f32[48,128]{1,0:T(8,128)} %get-tuple-element.6.cos_ref, f32[48,128]{1,0:T(8,128)} %get-tuple-element.5.sin_ref, f32[96,512]{1,0:T(8,128)} %compare_convert_fusion.mask_ref, f32[96,48]{1,0:T(8,128)} %bitcast.6, ...), custom_call_target="tpu_custom_call" | custom-call | tf_op jit(solution)/shard_map/pallas_call | solution.py:528
  112.0 1.1 reshape.98
  113.1 1.0 copy.27
  (6 shorter events, 0.0 us)
Async XLA Ops:
  12.0 5.9 %copy-start = (bf16[3584,448]{0,1:T(8,128)(2,1)S(1)}, bf16[3584,448]{0,1:T(8,128)(2,1)}, u32[]{:S(2)}) copy-start(bf16[3584,448]{0,1:T(8,128)(2,1)} %param.24) | copy-start | bytes 9633796

commit v2 on v1

--- a/solution.py
+++ b/solution.py
@@ -147,21 +147,23 @@
 
 
 def kernel(
-    x_ref, cos_ref, sin_ref, mask_ref, fresh_mask_ref, g1_ref, g2_ref, g3_ref, g4_ref,
+    x_ref, cos_ref, sin_ref, owner_ref, g1_ref, g2_ref, g3_ref, g4_ref,
     pw_hbm, ck_hbm, cv_hbm, ow_hbm, gw_hbm, uw_hbm, dw_hbm,
     out_ref,
     pw, ck, cv, ow, gw, uw, dw,
-    gbuf, bsend, brecv, tot_ref, tsend, trecv, csend, crecv, mid_ref, feed, lhs_ref, hid_ref,
+    xs_ref, res_ref, gbuf, bsend, brecv, tot_ref, tsend, trecv, csend, crecv, mid_ref, feed, lhs_ref, hid_ref,
     part_ref, e1send, e1recv, e2send, e2recv, e3send, e3recv,
-    load_sem, a_send, a_recv, b_send, b_recv, t_send, t_recv, c_send, c_recv,
-    d_send, d_recv, d2_send, d2_recv, e1_ssem, e1_rsem, e2_ssem, e2_rsem, e3_ssem, e3_rsem,
-    f_send, f_recv,
+    load_sem, a_send, a_recv, a_fwd, b_send, b_recv, t_send, t_recv, c_send, c_recv,
+    d_send, d_recv, d_fwd, d2_send, d2_recv, e1_ssem, e1_rsem, e2_ssem, e2_rsem, e3_ssem, e3_rsem,
+    f_send, f_recv, f_fwd,
 ):
     me = lax.axis_index("seq")
     row = lax.axis_index("req")
     width = x_ref.shape[2]
     rows = OWNERS * TILE
-    ff = gw.shape[1]
+    ff = gw.shape[0]
+    slots, steps = x_ref.shape[:2]
+    across = me + 1 - 2 * lax.rem(me, 2)
     other_core = row + 1 - 2 * lax.rem(row, 2)
     other_y = lax.rem(row + 2, REQ)
     is_owner = (me >= 1) & (me <= OWNERS)
@@ -195,39 +197,70 @@
 
     def rms(values, gain):
         mean_square = jnp.mean(values * values, axis=-1, keepdims=True)
-        return values * lax.rsqrt(mean_square + epsilon) * gain
-
-    stream = x_ref[...].astype(jnp.float32).reshape(rows, width)
-    normed = rms(stream, g1_ref[...]).astype(jnp.bfloat16)
-    loads[0].wait()
-    projected = jnp.dot(normed, pw[...], preferred_element_type=jnp.float32)
-    projected = projected.astype(jnp.bfloat16).astype(jnp.float32)
+        return values * lax.rsqrt(mean_square + epsilon) * gain[None, :]
+
+    for n in range(slots):
+        xs_ref[n * steps : (n + 1) * steps, :] = x_ref[n].astype(jnp.float32)
+    normed = rms(xs_ref[...], g1_ref[...]).astype(jnp.bfloat16)
     cosine, sine = cos_ref[...], sin_ref[...]
     half = HD // 2
-    for h in range(pw.shape[1] // HD):
-        a = projected[:, h * HD : h * HD + half]
-        b = projected[:, h * HD + half : (h + 1) * HD]
-        gbuf[me, :, h * HD : h * HD + half] = (a * cosine - b * sine).astype(jnp.bfloat16)
-        gbuf[me, :, h * HD + half : (h + 1) * HD] = (b * cosine + a * sine).astype(jnp.bfloat16)
-    pl.semaphore_wait(barrier, SEQ + 1)
-
-    def a_copy(d):
-        return remote(
-            gbuf.at[me], gbuf.at[me], a_send.at[d - 1], a_recv.at[me],
-            {"seq": lax.rem(me + d, SEQ)},
-        )
-
-    for d in range(1, SEQ):
-        a_copy(d).start()
-    for d in range(1, SEQ):
-        source = lax.rem(me + d, SEQ)
+    loads[0].wait()
+
+    def a_copy(part, k):
+        target = lax.rem(me + 2 * k, SEQ) if k else across
+        return remote(
+            gbuf.at[me, part], gbuf.at[me, part], a_send.at[part, k], a_recv.at[me, part],
+            {"seq": target},
+        )
+
+    def a_forward(part, k):
+        source = lax.rem(me + 2 * k, SEQ)
+        return remote(
+            gbuf.at[source, part], gbuf.at[source, part], a_fwd.at[part, k - 1],
+            a_recv.at[source, part], {"seq": across},
+        )
+
+    def a_arrived(source, part):
         remote(
-            gbuf.at[source], gbuf.at[source], a_send.at[d - 1], a_recv.at[source], {"seq": source}
+            gbuf.at[source, part], gbuf.at[source, part], a_fwd.at[0, 0],
+            a_recv.at[source, part], {"seq": across},
         ).wait_recv()
+
+    for part in range(2):
+        projected = jnp.dot(
+            normed, pw[:, part * 2 * HD : (part + 1) * 2 * HD], preferred_element_type=jnp.float32
+        )
+        projected = projected.astype(jnp.bfloat16).astype(jnp.float32)
+        for h in range(2):
+            a = projected[:, h * HD : h * HD + half]
+            b = projected[:, h * HD + half : (h + 1) * HD]
+            gbuf[me, part, :, h * HD : h * HD + half] = (a * cosine - b * sine).astype(
+                jnp.bfloat16
+            )
+            gbuf[me, part, :, h * HD + half : (h + 1) * HD] = (b * cosine + a * sine).astype(
+                jnp.bfloat16
+            )
+        if part == 0:
+            pl.semaphore_wait(barrier, SEQ + 1)
+        for k in (2, 3, 1, 0):
+            a_copy(part, k).start()
+    for part in range(2):
+        for k in range(1, 4):
+            a_arrived(lax.rem(me + 2 * k, SEQ), part)
+            a_forward(part, k).start()
 
     loads[1].wait()
     loads[2].wait()
-    owned = mask_ref[...] > 0.5
+    tokens = ck.shape[0]
+
+    def pair_row(shape, axis):
+        index = lax.broadcasted_iota(jnp.int32, shape, axis)
+        return jnp.where(index >= rows, index - rows, index)
+
+    owned = owner_ref[...] == pair_row((2 * rows, tokens), 0) // steps
+    query_row = pair_row((2 * rows, rows), 0)
+    fresh_row = lax.broadcasted_iota(jnp.int32, (2 * rows, rows), 1)
+    fresh_allowed = (query_row // steps == fresh_row // steps) & (fresh_row <= query_row)
     lanes = lax.broadcasted_iota(jnp.int32, (2 * rows, 128), 1)
     totals = jnp.zeros((2 * rows, 128), jnp.float32)
 
@@ -256,20 +289,29 @@
     for j in range(1, SEQ + 1):
         e = lax.rem(me + j, SEQ)
         block = e // 2
-        first = pl.multiple_of(lax.rem(e, 2) * (2 * HD), 2 * HD)
-        queries = jnp.concatenate(
-            [gbuf[block, :, pl.ds(first, HD)], gbuf[block, :, pl.ds(first + HD, HD)]], axis=0
-        )
+        part = lax.rem(e, 2)
+
+        @pl.when(lax.rem(block, 2) != lax.rem(me, 2))
+        def _():
+            a_arrived(block, part)
+
+        queries = jnp.concatenate([gbuf[block, part, :, :HD], gbuf[block, part, :, HD:]], axis=0)
         head = pl.ds(pl.multiple_of(e * HD, HD), HD)
         total, outputs = attend(queries, ck[:, head], cv[:, head], owned)
         if j < SEQ:
             bsend[j - 1] = outputs.astype(jnp.bfloat16)
             b_copy(j).start()
         else:
-            fresh = pl.ds(pl.multiple_of(lax.rem(e, 4) * HD, HD), HD)
+            for n in range(SEQ // 2, SEQ):
+                @pl.when(n % 2 != lax.rem(me, 2))
+                def _():
+                    a_arrived(n, 0)
+                    a_arrived(n, 1)
+
+            home, lane = lax.rem(e // 2, 2), pl.ds(pl.multiple_of(lax.rem(e, 2) * HD, HD), HD)
             fresh_total, fresh_outputs = attend(
-                queries, gbuf[4 + e // 4, :, fresh], gbuf[6 + e // 4, :, fresh],
-                fresh_mask_ref[...] > 0.5,
+                queries, gbuf[4 + e // 4, home, :, lane], gbuf[6 + e // 4, home, :, lane],
+                fresh_allowed,
             )
             total = total + fresh_total
             outputs = outputs + fresh_outputs
@@ -313,10 +355,20 @@
             pred, copy = c_send_to(c, d)
             pl.when(pred)(copy.start)
 
-    def d_copy(d):
-        return remote(
-            feed.at[0, mine], feed.at[0, mine], d_send.at[d - 1], d_recv.at[mine],
-            {"seq": lax.rem(me + d, SEQ)},
+    def d_copy(k):
+        target = lax.rem(me + 2 * k, SEQ) if k else across
+        return remote(
+            feed.at[0, mine], feed.at[0, mine], d_send.at[k], d_recv.at[mine], {"seq": target}
+        )
+
+    def owner_of(seq):
+        valid = (seq >= 1) & (seq <= OWNERS)
+        return valid, jnp.minimum(jnp.maximum(seq - 1, 0), OWNERS - 1)
+
+    def d_forward(k):
+        valid, o = owner_of(lax.rem(me + 2 * k, SEQ))
+        return valid, o, remote(
+            feed.at[0, o], feed.at[0, o], d_fwd.at[k - 1], d_recv.at[o], {"seq": across}
         )
 
     @pl.when(is_owner)
@@ -329,11 +381,11 @@
                 piece = piece + crecv[c, d - 1].astype(jnp.float32)
             pieces.append(piece)
         mixed = jnp.concatenate(pieces, axis=1)
-        middle = x_ref[mine].astype(jnp.float32) + rms(mixed, g2_ref[...])
+        middle = xs_ref[pl.ds(pl.multiple_of(mine * TILE, TILE), TILE), :] + rms(mixed, g2_ref[...])
         mid_ref[...] = middle
         feed[0, mine] = rms(middle, g3_ref[...]).astype(jnp.bfloat16)
-        for d in range(1, SEQ):
-            d_copy(d).start()
+        for k in (2, 3, 1, 0):
+            d_copy(k).start()
 
     def to_y(o):
         return remote(
@@ -350,32 +402,60 @@
             feed.at[2, o], feed.at[3, o], d2_send.at[2, o], d2_recv.at[2, o], {"req": other_core}
         )
 
-    for o in range(OWNERS):
-        @pl.when(me != o + 1)
+    def fill(q):
+        lhs_ref[q * rows : (q + 1) * rows, :] = (
+            feed[q].astype(jnp.float32).reshape(rows, width).astype(jnp.bfloat16)
+        )
+
+    def feed_half(n):
+        block = lhs_ref[n * 2 * rows : (n + 1) * 2 * rows, :]
+        nt = (((1,), (1,)), ((), ()))
+        gate_part = lax.dot_general(block, gw[...], nt, preferred_element_type=jnp.float32)
+        up_part = lax.dot_general(block, uw[...], nt, preferred_element_type=jnp.float32)
+        hidden = (jax.nn.gelu(gate_part, approximate=True) * up_part).astype(jnp.bfloat16)
+        hid_ref[n * 2 * rows : (n + 1) * 2 * rows, :ff] = hidden
+
+    @pl.when(is_owner)
+    def _():
+        to_y(mine).start()
+        to_core(mine).start()
+
+    for k in range(1, 4):
+        valid, o, copy = d_forward(k)
+
+        @pl.when(valid)
+        def _():
+            copy.wait_recv()
+            copy.start()
+            to_y(o).start()
+            to_core(o).start()
+
+    for k in range(4):
+        valid, o = owner_of(lax.rem(across + 2 * k, SEQ))
+
+        @pl.when(valid)
         def _():
             remote(
-                feed.at[0, o], feed.at[0, o], d_send.at[0], d_recv.at[o], {"seq": o + 1}
+                feed.at[0, o], feed.at[0, o], d_fwd.at[0], d_recv.at[o], {"seq": across}
             ).wait_recv()
-
-        to_y(o).start()
-        to_core(o).start()
+            to_y(o).start()
+            to_core(o).start()
+
+    fill(0)
+    for o in range(OWNERS):
+        to_core(o).wait_recv()
+    fill(1)
+    loads[4].wait()
+    loads[5].wait()
+    feed_half(0)
     for o in range(OWNERS):
         to_y(o).wait_recv()
         to_corner(o).start()
+    fill(2)
     for o in range(OWNERS):
-        to_core(o).wait_recv()
         to_corner(o).wait_recv()
-
-    for q in range(REQ):
-        lhs_ref[q * rows : (q + 1) * rows, :] = (
-            feed[q].astype(jnp.float32).reshape(rows, width).astype(jnp.bfloat16)
-        )
-    loads[4].wait()
-    loads[5].wait()
-    gate_part = jnp.dot(lhs_ref[...], gw[...], preferred_element_type=jnp.float32)
-    up_part = jnp.dot(lhs_ref[...], uw[...], preferred_element_type=jnp.float32)
-    hidden = (jax.nn.gelu(gate_part, approximate=True) * up_part).astype(jnp.bfloat16)
-    hid_ref[:, :ff] = hidden
+    fill(3)
+    feed_half(1)
     loads[6].wait()
     piece_width = width // SUM_CHUNKS
 
@@ -422,10 +502,16 @@
             pred, copy = e3_copy(c, d)
             pl.when(pred)(copy.start)
 
-    def f_copy(d):
-        return remote(
-            out_ref.at[mine], out_ref.at[mine], f_send.at[d - 1], f_recv.at[mine],
-            {"seq": lax.rem(me + d, SEQ)},
+    def f_copy(k):
+        target = lax.rem(me + 2 * k, SEQ) if k else across
+        return remote(
+            res_ref.at[mine], res_ref.at[mine], f_send.at[k], f_recv.at[mine], {"seq": target}
+        )
+
+    def f_forward(k):
+        valid, o = owner_of(lax.rem(me + 2 * k, SEQ))
+        return valid, remote(
+            res_ref.at[o], res_ref.at[o], f_fwd.at[k - 1], f_recv.at[o], {"seq": across}
         )
 
     @pl.when(is_owner)
@@ -438,19 +524,32 @@
                 piece = piece + e3recv[c, d - 1].astype(jnp.float32)
             pieces.append(piece)
         summed = jnp.concatenate(pieces, axis=1)
-        out_ref[mine] = (mid_ref[...] + rms(summed, g4_ref[...])).astype(jnp.bfloat16)
-        for d in range(1, SEQ):
-            f_copy(d).start()
-
-    for o in range(OWNERS):
-        @pl.when(me != o + 1)
+        res_ref[mine] = (mid_ref[...] + rms(summed, g4_ref[...])).astype(jnp.bfloat16)
+        for k in (2, 3, 1, 0):
+            f_copy(k).start()
+
+    for k in range(1, 4):
+        valid, copy = f_forward(k)
+
+        @pl.when(valid)
+        def _():
+            copy.wait_recv()
+            copy.start()
+
+    for k in range(4):
+        valid, o = owner_of(lax.rem(across + 2 * k, SEQ))
+
+        @pl.when(valid)
         def _():
             remote(
-                out_ref.at[o], out_ref.at[o], f_send.at[0], f_recv.at[o], {"seq": o + 1}
+                res_ref.at[o], res_ref.at[o], f_fwd.at[0], f_recv.at[o], {"seq": across}
             ).wait_recv()
 
+    finished = res_ref[...].astype(jnp.float32).reshape(rows, width)
+    for n in range(slots):
+        out_ref[n] = finished[n * steps : (n + 1) * steps].astype(jnp.bfloat16)
+
     for d in range(1, SEQ):
-        a_copy(d).wait_send()
         b_copy(d).wait_send()
         t_copy(d).wait_send()
         for c in range(MIX_CHUNKS):
@@ -459,6 +558,16 @@
         for c in range(SUM_CHUNKS):
             pred, copy = e3_copy(c, d)
             pl.when(pred)(copy.wait_send)
+    for part in range(2):
+        for k in range(4):
+            a_copy(part, k).wait_send()
+        for k in range(1, 4):
+            a_forward(part, k).wait_send()
+    for k in range(1, 4):
+        valid, _o, copy = d_forward(k)
+        pl.when(valid)(copy.wait_send)
+        valid, copy = f_forward(k)
+        pl.when(valid)(copy.wait_send)
     for o in range(OWNERS):
         to_y(o).wait_send()
         to_core(o).wait_send()
@@ -469,9 +578,9 @@
 
     @pl.when(is_owner)
     def _():
-        for d in range(1, SEQ):
-            d_copy(d).wait_send()
-            f_copy(d).wait_send()
+        for k in range(4):
+            d_copy(k).wait_send()
+            f_copy(k).wait_send()
 
 
 def fused_body(
@@ -507,7 +616,7 @@
     slot_requests = lax.dynamic_slice_in_dim(dealing, group_index * row_count, row_count)
     matches = slot_requests[:, None] == jnp.arange(dealing.shape[0], dtype=jnp.int32)[None, :]
     base_positions = jnp.sum(jnp.where(matches, lengths[None, :], 0), axis=1)
-    positions = base_positions[None, :] + jnp.arange(STEPS, dtype=jnp.int32)[:, None]
+    positions = base_positions[:, None] + jnp.arange(STEPS, dtype=jnp.int32)[None, :]
     positions = positions.reshape(rows).astype(jnp.float32)
     freq_index = jnp.arange(HD // 2, dtype=jnp.float32)
     inverse = jnp.exp(freq_index * (-2.0 * math.log(10000.0) / HD))
@@ -516,29 +625,26 @@
     turned = seq_index < 3 * SEQ // 4
     cosine = jnp.where(turned, jnp.cos(angles) * scale, 1.0)
     sine = jnp.where(turned, jnp.sin(angles) * scale, 0.0)
-    slots = jnp.tile(jnp.arange(row_count, dtype=jnp.int32), STEPS)
-    moments = jnp.repeat(jnp.arange(STEPS, dtype=jnp.int32), row_count)
-    mask = (token_owner[0][None, :] == jnp.tile(slots, 2)[:, None]).astype(jnp.float32)
-    fresh_mask = (slots[None, :] == slots[:, None]) & (moments[None, :] <= moments[:, None])
-    fresh_mask = jnp.tile(fresh_mask, (2, 1)).astype(jnp.float32)
     bf16, f32 = jnp.bfloat16, jnp.float32
     dma = pltpu.SemaphoreType.DMA
     vmem = pl.BlockSpec(memory_space=pltpu.VMEM)
     hbm = pl.BlockSpec(memory_space=pl.ANY)
     out = pl.pallas_call(
         kernel,
-        out_shape=jax.ShapeDtypeStruct((OWNERS, TILE, width), bf16),
-        in_specs=[vmem] * 9 + [hbm] * 7,
+        out_shape=jax.ShapeDtypeStruct((row_count, STEPS, width), bf16),
+        in_specs=[vmem] * 8 + [hbm] * 7,
         out_specs=vmem,
         scratch_shapes=[
             pltpu.VMEM((width, columns), bf16),
             pltpu.VMEM((tokens, kvw), bf16),
             pltpu.VMEM((tokens, kvw), bf16),
             pltpu.VMEM((depth, width), bf16),
-            pltpu.VMEM((width, ff), bf16),
-            pltpu.VMEM((width, ff), bf16),
+            pltpu.VMEM((ff, width), bf16),
+            pltpu.VMEM((ff, width), bf16),
             pltpu.VMEM((ff_pad, width), bf16),
-            pltpu.VMEM((SEQ, rows, columns), bf16),
+            pltpu.VMEM((rows, width), f32),
+            pltpu.VMEM((OWNERS, TILE, width), bf16),
+            pltpu.VMEM((SEQ, 2, rows, columns // 2), bf16),
             pltpu.VMEM((SEQ - 1, 2 * rows, HD), bf16),
             pltpu.VMEM((SEQ - 1, 2 * rows, HD), bf16),
             pltpu.VMEM((128, 128), f32),
@@ -558,16 +664,18 @@
             pltpu.VMEM((SUM_CHUNKS, OWNERS, TILE, piece), bf16),
             pltpu.VMEM((SUM_CHUNKS, SEQ - 1, TILE, piece), bf16),
             dma((7,)),
-            dma((SEQ - 1,)),
-            dma((SEQ,)),
+            dma((2, 4)),
+            dma((SEQ, 2)),
+            dma((2, 3)),
             dma((SEQ - 1,)),
             dma((SEQ - 1,)),
             dma((SEQ - 1,)),
             dma((SEQ - 1,)),
             dma((MIX_CHUNKS, SEQ - 1)),
             dma((MIX_CHUNKS, SEQ - 1)),
-            dma((SEQ - 1,)),
+            dma((4,)),
             dma((OWNERS,)),
+            dma((3,)),
             dma((3, OWNERS)),
             dma((3, OWNERS)),
             dma((SUM_CHUNKS,)),
@@ -576,31 +684,31 @@
             dma((SUM_CHUNKS,)),
             dma((SUM_CHUNKS, SEQ - 1)),
             dma((SUM_CHUNKS, SEQ - 1)),
-            dma((SEQ - 1,)),
+            dma((4,)),
             dma((OWNERS,)),
+            dma((3,)),
         ],
         compiler_params=pltpu.CompilerParams(
             collective_id=0, has_side_effects=True, vmem_limit_bytes=58 << 20
         ),
     )(
-        embedded.reshape(OWNERS, TILE, width),
+        embedded.transpose(1, 0, 2),
         cosine,
         sine,
-        mask,
-        fresh_mask,
-        gain_first[None, :],
-        gain_second[None, :],
-        gain_third[None, :],
-        gain_fourth[None, :],
+        token_owner,
+        gain_first,
+        gain_second,
+        gain_third,
+        gain_fourth,
         project_weight,
         cache_keys[0],
         cache_values[0],
         output_weight,
-        gate_weight,
-        up_weight,
+        gate_weight.T,
+        up_weight.T,
         down_weight,
     )
-    return out.reshape(STEPS, row_count, width)
+    return out.transpose(1, 0, 2)
 
 
 def body(*args):

time: 116 us -> 89.3 us (0.77); the launches traced: 114 us -> 89.2 us
  local copies, waits for them, and re-layouts: 20.5 us -> 2.64 us
  Pallas kernels: 90.4 us -> 84.8 us
  other arithmetic: 3.15 us -> 1.72 us
    unnamed x5 -> x1, local copies, waits for them, and re-layouts: 10.6 us -> 1.83 us
    pallas_call x1, Pallas kernels: 90.4 us -> 84.8 us  [fused_body(): pl.pallas_call(kernel, out_shape=jax.ShapeDtypeStruct((row_count, STEPS,...]
    broadcast_in_dim x4 -> x0, local copies, waits for them, and re-layouts: 5.31 us -> none  [the longest x1 1.33 us: fused_body(): gain_fourth[None, :]]
    reshape x3 -> x0, local copies, waits for them, and re-layouts: 2.87 us -> none  [the longest x2 2.06 us: fused_body(): return out.reshape(STEPS, row_count, width)]
    convert_element_type x2 -> x0, other arithmetic: 1.5 us -> none  [the longest x1 1.43 us: fused_body(): (token_owner[0][None, :] == jnp.tile(slots, 2)[:, None]).astype(jnp.float32)]
where the time goes in v2:
time: 89.3 us; the launch traced here: 89.2 us
  Pallas kernels  84.8 us (95%)
  local copies, waits for them, and re-layouts  2.64 us (3%)
  other arithmetic  1.72 us (2%)
    pallas_call x1, Pallas kernels, fused_body(): pl.pallas_call(kernel, out_shape=jax.ShapeDtypeStruct((row_count, STEPS,...  84.8 us
    unnamed x1, local copies, waits for them, and re-layouts  1.83 us

profile of v2, /device:TPU:0, one launch (start us, length us, event | category | flops | bytes accessed | tf_op | source)
XLA Modules:
  0.0 89.2 jit_solution(2117106194205991524)
XLA Ops:
  0.0 0.7 dynamic_slice.3
  0.7 0.8 select_reduce_fusion
  1.6 0.1 add_convert_fusion
  1.6 0.1 convert_element_type.11
  1.7 0.8 fusion.3
  2.5 84.8 %shard_map.145 = bf16[12,4,3584]{2,1,0:T(4,128)(2,1)} custom-call(bf16[12,4,3584]{2,1,0:T(4,128)(2,1)} %bitcast.11, f32[48,128]{1,0:T(8,128)} %get-tuple-element.6.cos_ref, f32[48,128]{1,0:T(8,128)} %get-tuple-element.5.sin_ref, s32[1,512]{1,0:T(1,128)} %owner_ref.1, f32[3584]{0:T(1024)} %g1_ref.1, f32[3584]{0:T(1024)} %g2_ref.1, f32[3584]{0:T(1024)} %g3_ref.1, ...), custom_call_target="tpu_custom_call" | custom-call | tf_op jit(solution)/shard_map/pallas_call | solution.py:632
  87.3 1.8 %copy.17 = bf16[4,12,3584]{2,0,1:T(4,128)(2,1)} copy(bf16[4,12,3584]{2,0,1:T(4,128)(2,1)} %bitcast.10) | data formatting | bytes 688128
  (1 shorter events, 0.0 us)

commit v3 on v2

--- a/solution.py
+++ b/solution.py
@@ -151,9 +151,9 @@
     pw_hbm, ck_hbm, cv_hbm, ow_hbm, gw_hbm, uw_hbm, dw_hbm,
     out_ref,
     pw, ck, cv, ow, gw, uw, dw,
-    xs_ref, res_ref, gbuf, bsend, brecv, tot_ref, tsend, trecv, csend, crecv, mid_ref, feed, lhs_ref, hid_ref,
+    xs_ref, res_ref, gbuf, bsend, brecv, bzsend, bzrecv, tot_ref, tsend, trecv, csend, crecv, mid_ref, feed, lhs_ref, hid_ref,
     part_ref, e1send, e1recv, e2send, e2recv, e3send, e3recv,
-    load_sem, a_send, a_recv, a_fwd, b_send, b_recv, t_send, t_recv, c_send, c_recv,
+    load_sem, a_send, a_recv, a_fwd, b_send, b_recv, bz_send, bz_recv, t_send, t_recv, c_send, c_recv,
     d_send, d_recv, d_fwd, d2_send, d2_recv, e1_ssem, e1_rsem, e2_ssem, e2_rsem, e3_ssem, e3_rsem,
     f_send, f_recv, f_fwd,
 ):
@@ -172,14 +172,16 @@
     loads = [
         pltpu.make_async_copy(src, dst, load_sem.at[n])
         for n, (src, dst) in enumerate(
-            [(pw_hbm, pw), (ck_hbm, ck), (cv_hbm, cv), (ow_hbm, ow), (gw_hbm, gw), (uw_hbm, uw)]
+            [(pw_hbm.at[:, pl.ds(0, 2 * HD)], pw.at[0]), (ck_hbm, ck), (cv_hbm, cv), (ow_hbm, ow),
+             (gw_hbm, gw), (uw_hbm, uw)]
         )
     ]
-    dw[ff:, :] = jnp.zeros((dw.shape[0] - ff, width), dw.dtype)
-    hid_ref[...] = jnp.zeros_like(hid_ref)
     loads.append(pltpu.make_async_copy(dw_hbm, dw.at[pl.ds(0, ff)], load_sem.at[6]))
-    for load in loads:
-        load.start()
+    loads.append(
+        pltpu.make_async_copy(pw_hbm.at[:, pl.ds(2 * HD, 2 * HD)], pw.at[1], load_sem.at[7])
+    )
+    loads[0].start()
+    loads[7].start()
 
     barrier = pltpu.get_barrier_semaphore()
     for d in range(1, SEQ):
@@ -204,7 +206,8 @@
     normed = rms(xs_ref[...], g1_ref[...]).astype(jnp.bfloat16)
     cosine, sine = cos_ref[...], sin_ref[...]
     half = HD // 2
-    loads[0].wait()
+    dw[ff:, :] = jnp.zeros((dw.shape[0] - ff, width), dw.dtype)
+    hid_ref[...] = jnp.zeros_like(hid_ref)
 
     def a_copy(part, k):
         target = lax.rem(me + 2 * k, SEQ) if k else across
@@ -227,9 +230,11 @@
         ).wait_recv()
 
     for part in range(2):
-        projected = jnp.dot(
-            normed, pw[:, part * 2 * HD : (part + 1) * 2 * HD], preferred_element_type=jnp.float32
-        )
+        loads[7 if part else 0].wait()
+        if part:
+            for n in range(1, 7):
+                loads[n].start()
+        projected = jnp.dot(normed, pw[part], preferred_element_type=jnp.float32)
         projected = projected.astype(jnp.bfloat16).astype(jnp.float32)
         for h in range(2):
             a = projected[:, h * HD : h * HD + half]
@@ -274,10 +279,13 @@
         )
         return jnp.sum(weights, axis=-1, keepdims=True), outputs
 
-    def b_copy(j):
-        return remote(
-            bsend.at[j - 1], brecv.at[j - 1], b_send.at[j - 1], b_recv.at[j - 1],
-            {"seq": lax.rem(me + j, SEQ)},
+    def b_copy(k):
+        return remote(bsend.at[k], brecv.at[k], b_send.at[k], b_recv.at[k], {"seq": across})
+
+    def bz_copy(k):
+        return remote(
+            bzsend.at[k - 1], bzrecv.at[k - 1], bz_send.at[k - 1], bz_recv.at[k - 1],
+            {"seq": lax.rem(me + 2 * k, SEQ)},
         )
 
     def t_copy(j):
@@ -286,8 +294,9 @@
             {"seq": lax.rem(me + j, SEQ)},
         )
 
-    for j in range(1, SEQ + 1):
-        e = lax.rem(me + j, SEQ)
+    for side, k in [(across, 2), (across, 3), (across, 1), (across, 0),
+                    (me, 2), (me, 3), (me, 1), (me, 0)]:
+        e = lax.rem(side + 2 * k, SEQ)
         block = e // 2
         part = lax.rem(e, 2)
 
@@ -298,9 +307,13 @@
         queries = jnp.concatenate([gbuf[block, part, :, :HD], gbuf[block, part, :, HD:]], axis=0)
         head = pl.ds(pl.multiple_of(e * HD, HD), HD)
         total, outputs = attend(queries, ck[:, head], cv[:, head], owned)
-        if j < SEQ:
-            bsend[j - 1] = outputs.astype(jnp.bfloat16)
-            b_copy(j).start()
+        if side is across:
+            bsend[k] = outputs.astype(jnp.bfloat16)
+            b_copy(k).start()
+        elif k:
+            b_copy(k).wait_recv()
+            bzsend[k - 1] = (outputs + brecv[k].astype(jnp.float32)).astype(jnp.bfloat16)
+            bz_copy(k).start()
         else:
             for n in range(SEQ // 2, SEQ):
                 @pl.when(n % 2 != lax.rem(me, 2))
@@ -322,10 +335,13 @@
     for j in range(1, SEQ):
         t_copy(j).start()
     everyone = tsend[...]
+    b_copy(0).wait_recv()
+    outputs = outputs + brecv[0].astype(jnp.float32)
+    for k in range(1, 4):
+        bz_copy(k).wait_recv()
+        outputs = outputs + bzrecv[k - 1].astype(jnp.float32)
     for j in range(1, SEQ):
-        b_copy(j).wait_recv()
         t_copy(j).wait_recv()
-        outputs = outputs + brecv[j - 1].astype(jnp.float32)
         everyone = everyone + trecv[j - 1]
     tot_ref[...] = jnp.zeros((128, 128), jnp.float32)
     tot_ref[:KVH, :] = everyone
@@ -550,7 +566,6 @@
         out_ref[n] = finished[n * steps : (n + 1) * steps].astype(jnp.bfloat16)
 
     for d in range(1, SEQ):
-        b_copy(d).wait_send()
         t_copy(d).wait_send()
         for c in range(MIX_CHUNKS):
             pred, copy = c_send_to(c, d)
@@ -558,6 +573,10 @@
         for c in range(SUM_CHUNKS):
             pred, copy = e3_copy(c, d)
             pl.when(pred)(copy.wait_send)
+    for k in range(4):
+        b_copy(k).wait_send()
+    for k in range(1, 4):
+        bz_copy(k).wait_send()
     for part in range(2):
         for k in range(4):
             a_copy(part, k).wait_send()
@@ -635,7 +654,7 @@
         in_specs=[vmem] * 8 + [hbm] * 7,
         out_specs=vmem,
         scratch_shapes=[
-            pltpu.VMEM((width, columns), bf16),
+            pltpu.VMEM((2, width, columns // 2), bf16),
             pltpu.VMEM((tokens, kvw), bf16),
             pltpu.VMEM((tokens, kvw), bf16),
             pltpu.VMEM((depth, width), bf16),
@@ -645,8 +664,10 @@
             pltpu.VMEM((rows, width), f32),
             pltpu.VMEM((OWNERS, TILE, width), bf16),
             pltpu.VMEM((SEQ, 2, rows, columns // 2), bf16),
-            pltpu.VMEM((SEQ - 1, 2 * rows, HD), bf16),
-            pltpu.VMEM((SEQ - 1, 2 * rows, HD), bf16),
+            pltpu.VMEM((4, 2 * rows, HD), bf16),
+            pltpu.VMEM((4, 2 * rows, HD), bf16),
+            pltpu.VMEM((3, 2 * rows, HD), bf16),
+            pltpu.VMEM((3, 2 * rows, HD), bf16),
             pltpu.VMEM((128, 128), f32),
             pltpu.VMEM((KVH, 128), f32),
             pltpu.VMEM((SEQ - 1, KVH, 128), f32),
@@ -663,12 +684,14 @@
             pltpu.VMEM((SUM_CHUNKS, rows, piece), bf16),
             pltpu.VMEM((SUM_CHUNKS, OWNERS, TILE, piece), bf16),
             pltpu.VMEM((SUM_CHUNKS, SEQ - 1, TILE, piece), bf16),
-            dma((7,)),
+            dma((8,)),
             dma((2, 4)),
             dma((SEQ, 2)),
             dma((2, 3)),
-            dma((SEQ - 1,)),
-            dma((SEQ - 1,)),
+            dma((4,)),
+            dma((4,)),
+            dma((3,)),
+            dma((3,)),
             dma((SEQ - 1,)),
             dma((SEQ - 1,)),
             dma((MIX_CHUNKS, SEQ - 1)),

time: 89.3 us -> 86.2 us (0.965)
  Pallas kernels: 84.8 us -> 81.7 us
    pallas_call x1, Pallas kernels: 84.8 us -> 81.7 us  [fused_body(): pl.pallas_call(kernel, out_shape=jax.ShapeDtypeStruct((row_count, STEPS,...]
where the time goes in v3:
time: 86.2 us; the launch traced here: 86.1 us
  Pallas kernels  81.7 us (95%)
  local copies, waits for them, and re-layouts  2.64 us (3%)
  other arithmetic  1.72 us (2%)
    pallas_call x1, Pallas kernels, fused_body(): pl.pallas_call(kernel, out_shape=jax.ShapeDtypeStruct((row_count, STEPS,...  81.7 us
    unnamed x1, local copies, waits for them, and re-layouts  1.83 us

profile of v3, /device:TPU:0, one launch (start us, length us, event | category | flops | bytes accessed | tf_op | source)
XLA Modules:
  0.0 86.1 jit_solution(13390076437977324450)
XLA Ops:
  0.0 0.7 dynamic_slice.3
  0.7 0.8 select_reduce_fusion
  1.6 0.1 add_convert_fusion
  1.6 0.1 convert_element_type.11
  1.7 0.8 fusion.3
  2.5 81.7 %shard_map.145 = bf16[12,4,3584]{2,1,0:T(4,128)(2,1)} custom-call(bf16[12,4,3584]{2,1,0:T(4,128)(2,1)} %bitcast.11, f32[48,128]{1,0:T(8,128)} %get-tuple-element.6.cos_ref, f32[48,128]{1,0:T(8,128)} %get-tuple-element.5.sin_ref, s32[1,512]{1,0:T(1,128)} %owner_ref.1, f32[3584]{0:T(1024)} %g1_ref.1, f32[3584]{0:T(1024)} %g2_ref.1, f32[3584]{0:T(1024)} %g3_ref.1, ...), custom_call_target="tpu_custom_call" | custom-call | tf_op jit(solution)/shard_map/pallas_call | solution.py:651
  84.2 1.8 %copy.17 = bf16[4,12,3584]{2,0,1:T(4,128)(2,1)} copy(bf16[4,12,3584]{2,0,1:T(4,128)(2,1)} %bitcast.10) | data formatting | bytes 688128
  (1 shorter events, 0.0 us)

commit v4 on v3

--- a/solution.py
+++ b/solution.py
@@ -142,8 +142,8 @@
 REQ = 4
 OWNERS = 6
 TILE = 8
-MIX_CHUNKS = 2
-SUM_CHUNKS = 4
+MIX_CHUNKS = 4
+SUM_CHUNKS = 7
 
 
 def kernel(

time: 86.2 us -> 85.7 us (level)
  no operation moved by 1% of the time
where the time goes in v4:
time: 85.7 us; the launch traced here: 85.3 us
  Pallas kernels  80.9 us (94%)
  local copies, waits for them, and re-layouts  2.64 us (3%)
  other arithmetic  1.72 us (2%)
    pallas_call x1, Pallas kernels, fused_body(): pl.pallas_call(kernel, out_shape=jax.ShapeDtypeStruct((row_count, STEPS,...  80.9 us
    unnamed x1, local copies, waits for them, and re-layouts  1.83 us

profile of v4, /device:TPU:0, one launch (start us, length us, event | category | flops | bytes accessed | tf_op | source)
XLA Modules:
  0.0 85.3 jit_solution(5988279500392920828)
XLA Ops:
  0.0 0.7 dynamic_slice.3
  0.7 0.8 select_reduce_fusion
  1.6 0.1 add_convert_fusion
  1.6 0.1 convert_element_type.11
  1.7 0.8 fusion.3
  2.5 80.9 %shard_map.145 = bf16[12,4,3584]{2,1,0:T(4,128)(2,1)} custom-call(bf16[12,4,3584]{2,1,0:T(4,128)(2,1)} %bitcast.11, f32[48,128]{1,0:T(8,128)} %get-tuple-element.6.cos_ref, f32[48,128]{1,0:T(8,128)} %get-tuple-element.5.sin_ref, s32[1,512]{1,0:T(1,128)} %owner_ref.1, f32[3584]{0:T(1024)} %g1_ref.1, f32[3584]{0:T(1024)} %g2_ref.1, f32[3584]{0:T(1024)} %g3_ref.1, ...), custom_call_target="tpu_custom_call" | custom-call | tf_op jit(solution)/shard_map/pallas_call | solution.py:651
  83.5 1.8 %copy.17 = bf16[4,12,3584]{2,0,1:T(4,128)(2,1)} copy(bf16[4,12,3584]{2,0,1:T(4,128)(2,1)} %bitcast.10) | data formatting | bytes 688128
  (1 shorter events, 0.0 us)
